TPU v7x, 128 devices: a whole 4x4x4 slice. The times are simulated.
128 devices in a mesh: row: 8 (over z_lo, x), col: 16 (over y, z_hi, core).
Axes of the slice: x: 4, y: 4, z: 4 (z_hi: 2, z_lo: 2; z = z_hi * 2 + z_lo), core: 2. Of those that a mesh axis runs over, the one named last changes fastest.
Arguments:
- positions: float32 [3, 16384, 128], P(None, ('row', 'col')), may hold values from -6 to 6
- block_links: int32 [2, 16384], replicated, may hold values from 0 to 16383, as said below
- panel_points: int32 [8, 256], replicated, may hold values from 0 to 2097151
Outputs:
- smoothed: float32 [3, 32768, 128], P(None, ('row', 'col'))
- velocity: float32 [8, 3, 256], P('row', None, 'col')
Inputs may be any that keep to these rules, and one draw needn't show every extreme that they name: block_links[0, b] is an owner device, numbered in the order of row+col; block_links[1] is a permutation of the 16384 blocks whose cycles are the loops, and all blocks of one loop have one owner. The 128 blocks of one device, b // 128, include at most 2 of any one owner, and in every draw one owner has exactly 2 blocks on every device.
All inputs are finite; a program needn't handle non-finite values.
Results may differ from a plain program's by a relative error of at most 0.0003.
Values sent between devices are 32-bit elements; how exact they have to be, the bound alone decides.
A program may use at most 128 MiB of HBM per device.

v0:
```python
import math
import jax
import jax.numpy as jnp
from jax import lax
from jax.sharding import PartitionSpec as P

SWEEPS = 2
SMOOTH_RATE = 0.25
CORE_SQUARED = 0.01


def cross_three(left_vec, right_vec):
    return jnp.stack(
        [
            left_vec[1] * right_vec[2] - left_vec[2] * right_vec[1],
            left_vec[2] * right_vec[0] - left_vec[0] * right_vec[2],
            left_vec[0] * right_vec[1] - left_vec[1] * right_vec[0],
        ]
    )


def neighbours(points, next_slot, prev_slot):
    ahead = jnp.concatenate([points[:, :, 1:], points[:, next_slot, :1]], axis=2)
    behind = jnp.concatenate([points[:, prev_slot, -1:], points[:, :, :-1]], axis=2)
    return (behind, ahead)


def smooth_loops(points, next_slot, prev_slot):
    for sweep_no in range(SWEEPS):
        behind, ahead = neighbours(points, next_slot, prev_slot)
        points = points + SMOOTH_RATE * (behind - 2.0 * points + ahead)
    return points


def panel_sums(targets, sources):
    centres = sources[:3]
    segments = sources[3:]
    inner = lax.dot_general(
        targets, centres, (((0,), (0,)), ((), ())), precision=lax.Precision.HIGHEST
    )
    squared = (
        jnp.sum(targets * targets, 0)[:, None]
        + jnp.sum(centres * centres, 0)[None, :]
        - 2.0 * inner
        + CORE_SQUARED
    )
    weights = 1.0 / (squared * jnp.sqrt(squared))
    features = jnp.concatenate([segments, cross_three(segments, centres)], 0)
    return lax.dot_general(
        weights, features, (((1,), (1,)), ((), ())), precision=lax.Precision.HIGHEST
    )


def tiled_sums(targets, piece, running, largest):
    blocks = piece.shape[1]
    block_len = piece.shape[2]
    group = max(
        [
            size_try
            for size_try in (1, 2, 4, 8, 16, 32, 64, 128)
            if blocks % size_try == 0 and size_try <= largest
        ]
    )

    def one_tile(turn, accum):
        tile = lax.dynamic_slice_in_dim(piece, turn * group, group, 1).reshape(6, group * block_len)
        return accum + panel_sums(targets, tile)

    return lax.fori_loop(0, blocks // group, one_tile, running)


def shards(positions, block_links, panel_points):
    devices = lax.axis_size(("row", "col"))
    my_index = lax.axis_index(("row", "col"))
    slots = positions.shape[1]
    block_len = positions.shape[2]
    capacity = 2 * slots // devices
    held_slots = devices * capacity
    owners = block_links[0]
    follows = block_links[1]
    blocks_all = owners.shape[0]
    counter = jnp.arange(blocks_all, dtype=jnp.int32)
    precedes = jnp.zeros_like(follows).at[follows].set(counter)
    owner_grid = owners.reshape(devices, slots)
    same_owner = owner_grid[:, :, None] == owner_grid[:, None, :]
    earlier = jnp.arange(slots)[None, :] < jnp.arange(slots)[:, None]
    ranks = jnp.sum(jnp.logical_and(same_owner, earlier[None]), axis=2).reshape(blocks_all)
    places = counter // slots * capacity + ranks
    my_owner = lax.dynamic_slice_in_dim(owners, my_index * slots, slots)
    my_rank = lax.dynamic_slice_in_dim(ranks, my_index * slots, slots)
    outgoing_slot = my_owner * capacity + my_rank
    outgoing = (
        jnp.zeros((3, held_slots, block_len), jnp.float32).at[:, outgoing_slot, :].set(positions)
    )
    arrived = lax.all_to_all(outgoing, ("row", "col"), split_axis=1, concat_axis=1, tiled=True)
    is_owned = owners == my_index
    held_ids = (
        jnp.full((held_slots,), blocks_all, jnp.int32)
        .at[jnp.where(is_owned, places, held_slots)]
        .set(counter, mode="drop")
    )
    live = held_ids < blocks_all
    safe_ids = jnp.minimum(held_ids, blocks_all - 1)
    slot_index = jnp.arange(held_slots, dtype=jnp.int32)
    next_slot = jnp.where(live, places[follows[safe_ids]], slot_index)
    prev_slot = jnp.where(live, places[precedes[safe_ids]], slot_index)
    smoothed = smooth_loops(arrived, next_slot, prev_slot)
    behind, ahead = neighbours(smoothed, next_slot, prev_slot)
    segments = ahead - smoothed
    centres = 0.5 * (ahead + smoothed)
    sources = jnp.concatenate([centres, segments], 0)
    wanted = panel_points.reshape(-1)
    wanted_block = wanted // block_len
    wanted_point = wanted % block_len
    wanted_mine = owners[wanted_block] == my_index
    picked = smoothed[:, places[wanted_block], wanted_point]
    local_targets = jnp.where(wanted_mine[None, :], picked, 0.0)
    all_targets = lax.psum(local_targets, ("row", "col"))
    panel = panel_points.shape[1]
    col_count = lax.axis_size("col")
    share = panel // col_count
    scale = 1.0 / (math.pi * math.sqrt(blocks_all * block_len))
    targets = lax.dynamic_slice_in_dim(all_targets, lax.axis_index("row") * panel, panel, 1)
    zero_sums = jnp.zeros((panel, 6), jnp.float32)
    sums = tiled_sums(targets, lax.all_gather(sources, "row", axis=1, tiled=True), zero_sums, 128)
    partial_velocity = scale * (cross_three(sums[:, :3].T, targets) - sums[:, 3:].T)
    summed = lax.psum(partial_velocity, "col")
    velocity_part = lax.dynamic_slice_in_dim(summed, lax.axis_index("col") * share, share, 1)
    return (smoothed, velocity_part[None])


def solution(mesh):
    placed = (P(None, ("row", "col"), None), P(), P())
    return jax.shard_map(
        shards,
        mesh=mesh,
        in_specs=placed,
        out_specs=(P(None, ("row", "col"), None), P("row", None, "col")),
        check_vma=False,
    )
```

profile of v0, /device:TPU:0, one launch (start us, length us, event | category | flops | bytes accessed | tf_op | source)
XLA Modules:
  0.0 976.3 jit_solution(4487103491891929501)
XLA Ops:
  15.4 12.5 %scatter_fusion = f32[3,256,128]{2,0,1:T(4,128)} fusion(f32[3,256,128]{2,0,1:T(4,128)} %broadcast_in_dim.36, s32[128]{0:T(128)S(1)} %compare_select_fusion.13, f32[128,3,128]{2,1,0:T(4,128)S(1)} %copy.77), kind=kCustom, calls=%fused_computation.12 | custom fusion | bytes 590336 | tf_op jit(solution)/shard_map/scatter | solution.py:93
  40.4 60.3 %scatter_custom_fusion.1 = s32[256]{0:T(256)S(1)} fusion(s32[16384]{0:T(1024)S(1)} %bitcast.119, s32[16384]{0:T(1024)S(1)} %iota.31, s32[]{:T(128)} %constant.150.clone.1), kind=kCustom, calls=%fused_computation.120 | custom fusion | bytes 1028 | tf_op jit(solution)/shard_map/scatter | solution.py:100
  100.8 60.5 %scatter_custom_fusion.2 = s32[16384]{0:T(1024)S(1)} fusion(s32[16384]{0:T(1024)S(1)} %bitcast.118, s32[16384]{0:T(1024)S(1)} %iota.33, s32[]{:T(128)} %constant.144.clone.1), kind=kCustom, calls=%fused_computation.79 | custom fusion | bytes 65540 | tf_op jit(solution)/shard_map/scatter | solution.py:83
  217.9 11.8 %gather_fusion.9 = s32[2048]{0:T(1024)S(1)} fusion(s32[16384]{0:T(1024)S(1)} %fusion.28, s32[2048]{0:T(1024)S(1)} %broadcast_clamp_fusion), kind=kCustom, calls=%fused_computation.9 | custom fusion | bytes 24576 | tf_op jit(solution)/shard_map/gather | solution.py:116
  242.3 20.8 %gather_fusion.10 = f32[2048,3]{1,0:T(8,128)S(1)} fusion(f32[3,256,128]{0,2,1:T(8,128)} %copy.90, s32[2048]{0:T(1024)S(1)} %bitcast.100), kind=kCustom, calls=%fused_computation.10 | custom fusion | bytes 65536 | tf_op jit(solution)/shard_map/gather | solution.py:116
  263.5 80.3 %psum.14 = f32[3,2048]{0,1:T(8,128)S(1)} all-reduce(f32[3,2048]{0,1:T(8,128)S(1)} %select_bitcast_fusion), channel_id=1, replica_groups=mesh['row'=8,'col'=16] {'row','col'}, use_global_device_ids=true, to_apply=%region_4.5 | all-reduce | flops 6144 | bytes 49152 | tf_op jit(solution)/shard_map/psum | solution.py:118
  344.3 586.7 %while.16 = (s32[]{:T(128)}, f32[256,6]{0,1:T(8,128)S(1)}, f32[256]{0:T(256)S(1)}, f32[6,2048,128]{2,1,0:T(8,128)}, f32[3,256]{1,0:T(4,128)S(1)}, /*index=5*/s32...) while((s32[]{:T(128)}, f32[256,6]{0,1:T(8,128)S(1)}, ...), condition=%wide.region_8.9_spmd.clone, body=%wide.region_6.8_spmd.clone.sunk | while | flops 478678016 | bytes 36061472 | solution.py:69
  346.8 25.7 %sqrt_multiply_fusion.2 = f32[256,16384]{0,1:T(8,128)S(1)} fusion(f32[3,256]{1,0:T(4,128)S(1)} %get-tuple-element.277, f32[16384]{0:T(1024)S(1)} %bitcast.107, f32[256]{0:T(256)S(1)} %get-tuple-element.275, f32[1,3,128,128]{3,2,1,0:T(8,128)S(1)} %get-tuple-element.240), kind=kOutput, calls=%fused_computation.15.clone.1 | convolution fusion | flops 171966464 | bytes 17043456 | tf_op jit(solution)/shard_map/while/body/eval_jaxpr/dot_general | solution.py:38
  383.4 25.7 %sqrt_multiply_fusion.2 = f32[256,16384]{0,1:T(8,128)S(1)} fusion(f32[3,256]{1,0:T(4,128)S(1)} %get-tuple-element.277, f32[16384]{0:T(1024)S(1)} %bitcast.107, f32[256]{0:T(256)S(1)} %get-tuple-element.275, f32[1,3,128,128]{3,2,1,0:T(8,128)S(1)} %get-tuple-element.240), kind=kOutput, calls=%fused_computation.15.clone.1 | convolution fusion | flops 171966464 | bytes 17043456 | tf_op jit(solution)/shard_map/while/body/eval_jaxpr/dot_general | solution.py:38
  420.1 25.7 %sqrt_multiply_fusion.2 = f32[256,16384]{0,1:T(8,128)S(1)} fusion(f32[3,256]{1,0:T(4,128)S(1)} %get-tuple-element.277, f32[16384]{0:T(1024)S(1)} %bitcast.107, f32[256]{0:T(256)S(1)} %get-tuple-element.275, f32[1,3,128,128]{3,2,1,0:T(8,128)S(1)} %get-tuple-element.240), kind=kOutput, calls=%fused_computation.15.clone.1 | convolution fusion | flops 171966464 | bytes 17043456 | tf_op jit(solution)/shard_map/while/body/eval_jaxpr/dot_general | solution.py:38
  456.8 25.7 %sqrt_multiply_fusion.2 = f32[256,16384]{0,1:T(8,128)S(1)} fusion(f32[3,256]{1,0:T(4,128)S(1)} %get-tuple-element.277, f32[16384]{0:T(1024)S(1)} %bitcast.107, f32[256]{0:T(256)S(1)} %get-tuple-element.275, f32[1,3,128,128]{3,2,1,0:T(8,128)S(1)} %get-tuple-element.240), kind=kOutput, calls=%fused_computation.15.clone.1 | convolution fusion | flops 171966464 | bytes 17043456 | tf_op jit(solution)/shard_map/while/body/eval_jaxpr/dot_general | solution.py:38
  493.4 25.7 %sqrt_multiply_fusion.2 = f32[256,16384]{0,1:T(8,128)S(1)} fusion(f32[3,256]{1,0:T(4,128)S(1)} %get-tuple-element.277, f32[16384]{0:T(1024)S(1)} %bitcast.107, f32[256]{0:T(256)S(1)} %get-tuple-element.275, f32[1,3,128,128]{3,2,1,0:T(8,128)S(1)} %get-tuple-element.240), kind=kOutput, calls=%fused_computation.15.clone.1 | convolution fusion | flops 171966464 | bytes 17043456 | tf_op jit(solution)/shard_map/while/body/eval_jaxpr/dot_general | solution.py:38
  530.1 25.7 %sqrt_multiply_fusion.2 = f32[256,16384]{0,1:T(8,128)S(1)} fusion(f32[3,256]{1,0:T(4,128)S(1)} %get-tuple-element.277, f32[16384]{0:T(1024)S(1)} %bitcast.107, f32[256]{0:T(256)S(1)} %get-tuple-element.275, f32[1,3,128,128]{3,2,1,0:T(8,128)S(1)} %get-tuple-element.240), kind=kOutput, calls=%fused_computation.15.clone.1 | convolution fusion | flops 171966464 | bytes 17043456 | tf_op jit(solution)/shard_map/while/body/eval_jaxpr/dot_general | solution.py:38
  566.7 25.7 %sqrt_multiply_fusion.2 = f32[256,16384]{0,1:T(8,128)S(1)} fusion(f32[3,256]{1,0:T(4,128)S(1)} %get-tuple-element.277, f32[16384]{0:T(1024)S(1)} %bitcast.107, f32[256]{0:T(256)S(1)} %get-tuple-element.275, f32[1,3,128,128]{3,2,1,0:T(8,128)S(1)} %get-tuple-element.240), kind=kOutput, calls=%fused_computation.15.clone.1 | convolution fusion | flops 171966464 | bytes 17043456 | tf_op jit(solution)/shard_map/while/body/eval_jaxpr/dot_general | solution.py:38
  603.4 25.7 %sqrt_multiply_fusion.2 = f32[256,16384]{0,1:T(8,128)S(1)} fusion(f32[3,256]{1,0:T(4,128)S(1)} %get-tuple-element.277, f32[16384]{0:T(1024)S(1)} %bitcast.107, f32[256]{0:T(256)S(1)} %get-tuple-element.275, f32[1,3,128,128]{3,2,1,0:T(8,128)S(1)} %get-tuple-element.240), kind=kOutput, calls=%fused_computation.15.clone.1 | convolution fusion | flops 171966464 | bytes 17043456 | tf_op jit(solution)/shard_map/while/body/eval_jaxpr/dot_general | solution.py:38
  640.0 25.7 %sqrt_multiply_fusion.2 = f32[256,16384]{0,1:T(8,128)S(1)} fusion(f32[3,256]{1,0:T(4,128)S(1)} %get-tuple-element.277, f32[16384]{0:T(1024)S(1)} %bitcast.107, f32[256]{0:T(256)S(1)} %get-tuple-element.275, f32[1,3,128,128]{3,2,1,0:T(8,128)S(1)} %get-tuple-element.240), kind=kOutput, calls=%fused_computation.15.clone.1 | convolution fusion | flops 171966464 | bytes 17043456 | tf_op jit(solution)/shard_map/while/body/eval_jaxpr/dot_general | solution.py:38
  676.7 25.7 %sqrt_multiply_fusion.2 = f32[256,16384]{0,1:T(8,128)S(1)} fusion(f32[3,256]{1,0:T(4,128)S(1)} %get-tuple-element.277, f32[16384]{0:T(1024)S(1)} %bitcast.107, f32[256]{0:T(256)S(1)} %get-tuple-element.275, f32[1,3,128,128]{3,2,1,0:T(8,128)S(1)} %get-tuple-element.240), kind=kOutput, calls=%fused_computation.15.clone.1 | convolution fusion | flops 171966464 | bytes 17043456 | tf_op jit(solution)/shard_map/while/body/eval_jaxpr/dot_general | solution.py:38
  713.4 25.7 %sqrt_multiply_fusion.2 = f32[256,16384]{0,1:T(8,128)S(1)} fusion(f32[3,256]{1,0:T(4,128)S(1)} %get-tuple-element.277, f32[16384]{0:T(1024)S(1)} %bitcast.107, f32[256]{0:T(256)S(1)} %get-tuple-element.275, f32[1,3,128,128]{3,2,1,0:T(8,128)S(1)} %get-tuple-element.240), kind=kOutput, calls=%fused_computation.15.clone.1 | convolution fusion | flops 171966464 | bytes 17043456 | tf_op jit(solution)/shard_map/while/body/eval_jaxpr/dot_general | solution.py:38
  750.0 25.7 %sqrt_multiply_fusion.2 = f32[256,16384]{0,1:T(8,128)S(1)} fusion(f32[3,256]{1,0:T(4,128)S(1)} %get-tuple-element.277, f32[16384]{0:T(1024)S(1)} %bitcast.107, f32[256]{0:T(256)S(1)} %get-tuple-element.275, f32[1,3,128,128]{3,2,1,0:T(8,128)S(1)} %get-tuple-element.240), kind=kOutput, calls=%fused_computation.15.clone.1 | convolution fusion | flops 171966464 | bytes 17043456 | tf_op jit(solution)/shard_map/while/body/eval_jaxpr/dot_general | solution.py:38
  786.7 25.7 %sqrt_multiply_fusion.2 = f32[256,16384]{0,1:T(8,128)S(1)} fusion(f32[3,256]{1,0:T(4,128)S(1)} %get-tuple-element.277, f32[16384]{0:T(1024)S(1)} %bitcast.107, f32[256]{0:T(256)S(1)} %get-tuple-element.275, f32[1,3,128,128]{3,2,1,0:T(8,128)S(1)} %get-tuple-element.240), kind=kOutput, calls=%fused_computation.15.clone.1 | convolution fusion | flops 171966464 | bytes 17043456 | tf_op jit(solution)/shard_map/while/body/eval_jaxpr/dot_general | solution.py:38
  823.3 25.7 %sqrt_multiply_fusion.2 = f32[256,16384]{0,1:T(8,128)S(1)} fusion(f32[3,256]{1,0:T(4,128)S(1)} %get-tuple-element.277, f32[16384]{0:T(1024)S(1)} %bitcast.107, f32[256]{0:T(256)S(1)} %get-tuple-element.275, f32[1,3,128,128]{3,2,1,0:T(8,128)S(1)} %get-tuple-element.240), kind=kOutput, calls=%fused_computation.15.clone.1 | convolution fusion | flops 171966464 | bytes 17043456 | tf_op jit(solution)/shard_map/while/body/eval_jaxpr/dot_general | solution.py:38
  860.0 25.7 %sqrt_multiply_fusion.2 = f32[256,16384]{0,1:T(8,128)S(1)} fusion(f32[3,256]{1,0:T(4,128)S(1)} %get-tuple-element.277, f32[16384]{0:T(1024)S(1)} %bitcast.107, f32[256]{0:T(256)S(1)} %get-tuple-element.275, f32[1,3,128,128]{3,2,1,0:T(8,128)S(1)} %get-tuple-element.240), kind=kOutput, calls=%fused_computation.15.clone.1 | convolution fusion | flops 171966464 | bytes 17043456 | tf_op jit(solution)/shard_map/while/body/eval_jaxpr/dot_general | solution.py:38
  896.7 25.7 %sqrt_multiply_fusion.2 = f32[256,16384]{0,1:T(8,128)S(1)} fusion(f32[3,256]{1,0:T(4,128)S(1)} %get-tuple-element.277, f32[16384]{0:T(1024)S(1)} %bitcast.107, f32[256]{0:T(256)S(1)} %get-tuple-element.275, f32[1,3,128,128]{3,2,1,0:T(8,128)S(1)} %get-tuple-element.240), kind=kOutput, calls=%fused_computation.15.clone.1 | convolution fusion | flops 171966464 | bytes 17043456 | tf_op jit(solution)/shard_map/while/body/eval_jaxpr/dot_general | solution.py:38
  931.7 37.0 %psum.15 = f32[3,256]{1,0:T(4,128)S(1)} all-reduce(f32[3,256]{1,0:T(4,128)S(1)} %fusion.41), channel_id=1, replica_groups=mesh['row'=8,'col'=16] {'col'}, use_global_device_ids=true, to_apply=%region_9.10 | all-reduce | flops 768 | bytes 6144 | tf_op jit(solution)/shard_map/psum | solution.py:127
  (137 shorter events, 267.6 us)
Async XLA Ops:
  27.9 140.4 %all-to-all-start = ((f32[3,256,128]{2,0,1:T(4,128)}), f32[3,256,128]{2,0,1:T(4,128)S(1)}, u32[]{:S(2)}, u32[]{:S(2)}) async-start(f32[3,256,128]{2,0,1:T(4,128)} %scatter_fusion), calls=%async_computation | async-start | bytes 1048576 | tf_op jit(solution)/shard_map/all_to_all | solution.py:95
  39.1 305.2 %all-gather.2.cloned.1.call-start = ((), (), s32[]{:S(2)}) async-start(), calls=%async_computation.1 | async-start | bytes 7077888 | tf_op jit(solution)/shard_map/all_gather | solution.py:125
  194.3 23.4 %copy-start = (s32[8,256]{1,0:T(8,128)S(1)}, s32[8,256]{1,0:T(8,128)}, u32[]{:S(2)}) copy-start(s32[8,256]{1,0:T(8,128)} %param.7) | copy-start | bytes 24580
Sparse Core Ops, SparseCore 0:
  217.9 75.4 all-gather.1
where the time goes:
time: 982 us; the launch traced here: 976 us
  matrix products  550 us (56%)
  local copies, waits for them, and re-layouts  239 us (24%)
  blocking collectives  117 us (12%)
  other arithmetic  42.8 us (4%)
  between operations  14.6 us (1%)
  starting transfers between devices  11.2 us (1%)
    dot_general x16, matrix products, panel_sums(): lax.dot_general(targets, centres, (((0,), (0,)), ((), ())), precision=lax...  410 us
    dot_general x16, matrix products, panel_sums(): lax.dot_general(weights, features, (((1,), (1,)), ((), ())), precision=la...  140 us
    psum x1, blocking collectives, shards(): all_targets = lax.psum(local_targets, ('row', 'col'))  80.3 us
    scatter x1, local copies, waits for them, and re-layouts, shards(): precedes = jnp.zeros_like(follows).at[follows].set(counter)  60.5 us
    scatter x1, local copies, waits for them, and re-layouts, shards(): held_ids = jnp.full((held_slots,), blocks_all, jnp.int32).at[jnp.where(is...  60.3 us
    psum x1, blocking collectives, shards(): summed = lax.psum(partial_velocity, 'col')  37 us
    gather x2, local copies, waits for them, and re-layouts, shards(): picked = smoothed[:, places[wanted_block], wanted_point]  32.6 us
  transfers between devices with their start and end apart: 2, of which 0 were waited for; matrix products, arithmetic and copies ran while one was open for 18% of the time, Pallas kernels for 0%

commit v1 on v0

--- a/solution.py
+++ b/solution.py
@@ -115,7 +115,7 @@
     wanted_mine = owners[wanted_block] == my_index
     picked = smoothed[:, places[wanted_block], wanted_point]
     local_targets = jnp.where(wanted_mine[None, :], picked, 0.0)
-    all_targets = lax.psum(local_targets, ("row", "col"))
+    all_targets = jnp.sum(lax.all_gather(local_targets, ("row", "col")), axis=0)
     panel = panel_points.shape[1]
     col_count = lax.axis_size("col")
     share = panel // col_count

time: 982 us -> 1170 us (1.19)
  waiting for transfers between devices: 0.02 us -> 261 us
  blocking collectives: 117 us -> 37.6 us
    all_gather x0 -> x1, waiting for transfers between devices: none -> 192 us  [shards(): all_targets = jnp.sum(lax.all_gather(local_targets, ('row', 'col')), axis=0)]
    psum x1 -> x0, blocking collectives: 80.3 us -> none  [shards(): all_targets = lax.psum(local_targets, ('row', 'col'))]
    all_gather x1, waiting for transfers between devices: 0.01 us -> 68.8 us  [shards(): lax.all_gather(sources, 'row', axis=1, tiled=True)]
  transfers between devices with their start and end apart: 2 -> 3, of which waited for: 0 -> 2; matrix products, arithmetic and copies ran while one was open for 18% -> 14% of each run, Pallas kernels for 0% -> 0%
where the time goes in v1:
time: 1170 us; the launch traced here: 1160 us
  matrix products  550 us (47%)
  waiting for transfers between devices  261 us (22%)
  local copies, waits for them, and re-layouts  241 us (21%)
  other arithmetic  44.6 us (4%)
  blocking collectives  37.6 us (3%)
  between operations  14.6 us (1%)
    dot_general x16, matrix products, panel_sums(): lax.dot_general(targets, centres, (((0,), (0,)), ((), ())), precision=lax...  410 us
    all_gather x1, waiting for transfers between devices, shards(): all_targets = jnp.sum(lax.all_gather(local_targets, ('row', 'col')), axis=0)  192 us
    dot_general x16, matrix products, panel_sums(): lax.dot_general(weights, features, (((1,), (1,)), ((), ())), precision=la...  140 us
    all_gather x1, waiting for transfers between devices, shards(): lax.all_gather(sources, 'row', axis=1, tiled=True)  68.8 us
    scatter x1, local copies, waits for them, and re-layouts, shards(): precedes = jnp.zeros_like(follows).at[follows].set(counter)  60.5 us
    scatter x1, local copies, waits for them, and re-layouts, shards(): held_ids = jnp.full((held_slots,), blocks_all, jnp.int32).at[jnp.where(is...  60.3 us
    psum x1, blocking collectives, shards(): summed = lax.psum(partial_velocity, 'col')  37.6 us
    gather x2, local copies, waits for them, and re-layouts, shards(): picked = smoothed[:, places[wanted_block], wanted_point]  32.8 us
  transfers between devices with their start and end apart: 3, of which 2 were waited for; matrix products, arithmetic and copies ran while one was open for 14% of the time, Pallas kernels for 0%

profile of v1, /device:TPU:0, one launch (start us, length us, event | category | flops | bytes accessed | tf_op | source)
XLA Modules:
  0.0 1161.3 jit_solution(13970231967604449137)
XLA Ops:
  15.5 12.5 %scatter_fusion = f32[3,256,128]{2,0,1:T(4,128)} fusion(f32[3,256,128]{2,0,1:T(4,128)} %broadcast_in_dim.36, s32[128]{0:T(128)S(1)} %compare_select_fusion.13, f32[128,3,128]{2,1,0:T(4,128)S(1)} %copy.97), kind=kCustom, calls=%fused_computation.12 | custom fusion | bytes 590336 | tf_op jit(solution)/shard_map/scatter | solution.py:93
  63.8 60.3 %scatter_custom_fusion.1 = s32[256]{0:T(256)S(1)} fusion(s32[16384]{0:T(1024)S(1)} %bitcast.121, s32[16384]{0:T(1024)S(1)} %iota.31, s32[]{:T(128)} %constant.150.clone.1), kind=kCustom, calls=%fused_computation.119 | custom fusion | bytes 1028 | tf_op jit(solution)/shard_map/scatter | solution.py:100
  124.2 60.5 %scatter_custom_fusion.2 = s32[16384]{0:T(1024)S(1)} fusion(s32[16384]{0:T(1024)S(1)} %bitcast.120, s32[16384]{0:T(1024)S(1)} %iota.33, s32[]{:T(128)} %constant.144.clone.1), kind=kCustom, calls=%fused_computation.79 | custom fusion | bytes 65540 | tf_op jit(solution)/shard_map/scatter | solution.py:83
  234.8 21.0 %gather_fusion.10 = f32[2048,3]{1,0:T(8,128)S(1)} fusion(f32[3,256,128]{0,2,1:T(8,128)} %copy.110, s32[2048]{0:T(1024)S(1)} %bitcast.102), kind=kCustom, calls=%fused_computation.10 | custom fusion | bytes 65536 | tf_op jit(solution)/shard_map/gather | solution.py:116
  264.0 192.5 %all-gather.3.cloned.1.call-done = f32[128,3,2048]{2,1,0:T(4,128)} async-done(((f32[1,3,2048]{2,1,0:T(4,128)}), f32[128,3,2048]{2,1,0:T(4,128)}) %all-gather.3.cloned.1.call-update) | async-done | bytes 3145744 | tf_op jit(solution)/shard_map/all_gather | solution.py:118
  460.0 68.8 %all-gather.5.cloned.1.call-done = f32[6,2048,128]{2,1,0:T(8,128)} async-done(((f32[6,256,128]{2,1,0:T(8,128)}), f32[6,2048,128]{2,1,0:T(8,128)}) %all-gather.5.cloned.1.call-update) | async-done | bytes 6291472 | tf_op jit(solution)/shard_map/all_gather | solution.py:125
  528.7 586.7 %while.16 = (s32[]{:T(128)}, f32[256,6]{0,1:T(8,128)S(1)}, f32[256]{0:T(256)S(1)}, f32[6,2048,128]{2,1,0:T(8,128)}, f32[3,256]{1,0:T(4,128)S(1)}, /*index=5*/s32...) while((s32[]{:T(128)}, f32[256,6]{0,1:T(8,128)S(1)}, ...), condition=%wide.region_8.9_spmd.clone, body=%wide.region_6.8_spmd.clone.sunk | while | flops 478678016 | bytes 36061472 | solution.py:69
  531.2 25.7 %sqrt_multiply_fusion.2 = f32[256,16384]{0,1:T(8,128)S(1)} fusion(f32[3,256]{1,0:T(4,128)S(1)} %get-tuple-element.282, f32[16384]{0:T(1024)S(1)} %bitcast.109, f32[256]{0:T(256)S(1)} %get-tuple-element.280, f32[1,3,128,128]{3,2,1,0:T(8,128)S(1)} %get-tuple-element.245), kind=kOutput, calls=%fused_computation.15.clone.1 | convolution fusion | flops 171966464 | bytes 17043456 | tf_op jit(solution)/shard_map/while/body/eval_jaxpr/dot_general | solution.py:38
  567.8 25.6 %sqrt_multiply_fusion.2 = f32[256,16384]{0,1:T(8,128)S(1)} fusion(f32[3,256]{1,0:T(4,128)S(1)} %get-tuple-element.282, f32[16384]{0:T(1024)S(1)} %bitcast.109, f32[256]{0:T(256)S(1)} %get-tuple-element.280, f32[1,3,128,128]{3,2,1,0:T(8,128)S(1)} %get-tuple-element.245), kind=kOutput, calls=%fused_computation.15.clone.1 | convolution fusion | flops 171966464 | bytes 17043456 | tf_op jit(solution)/shard_map/while/body/eval_jaxpr/dot_general | solution.py:38
  604.5 25.7 %sqrt_multiply_fusion.2 = f32[256,16384]{0,1:T(8,128)S(1)} fusion(f32[3,256]{1,0:T(4,128)S(1)} %get-tuple-element.282, f32[16384]{0:T(1024)S(1)} %bitcast.109, f32[256]{0:T(256)S(1)} %get-tuple-element.280, f32[1,3,128,128]{3,2,1,0:T(8,128)S(1)} %get-tuple-element.245), kind=kOutput, calls=%fused_computation.15.clone.1 | convolution fusion | flops 171966464 | bytes 17043456 | tf_op jit(solution)/shard_map/while/body/eval_jaxpr/dot_general | solution.py:38
  641.1 25.7 %sqrt_multiply_fusion.2 = f32[256,16384]{0,1:T(8,128)S(1)} fusion(f32[3,256]{1,0:T(4,128)S(1)} %get-tuple-element.282, f32[16384]{0:T(1024)S(1)} %bitcast.109, f32[256]{0:T(256)S(1)} %get-tuple-element.280, f32[1,3,128,128]{3,2,1,0:T(8,128)S(1)} %get-tuple-element.245), kind=kOutput, calls=%fused_computation.15.clone.1 | convolution fusion | flops 171966464 | bytes 17043456 | tf_op jit(solution)/shard_map/while/body/eval_jaxpr/dot_general | solution.py:38
  677.8 25.7 %sqrt_multiply_fusion.2 = f32[256,16384]{0,1:T(8,128)S(1)} fusion(f32[3,256]{1,0:T(4,128)S(1)} %get-tuple-element.282, f32[16384]{0:T(1024)S(1)} %bitcast.109, f32[256]{0:T(256)S(1)} %get-tuple-element.280, f32[1,3,128,128]{3,2,1,0:T(8,128)S(1)} %get-tuple-element.245), kind=kOutput, calls=%fused_computation.15.clone.1 | convolution fusion | flops 171966464 | bytes 17043456 | tf_op jit(solution)/shard_map/while/body/eval_jaxpr/dot_general | solution.py:38
  714.5 25.7 %sqrt_multiply_fusion.2 = f32[256,16384]{0,1:T(8,128)S(1)} fusion(f32[3,256]{1,0:T(4,128)S(1)} %get-tuple-element.282, f32[16384]{0:T(1024)S(1)} %bitcast.109, f32[256]{0:T(256)S(1)} %get-tuple-element.280, f32[1,3,128,128]{3,2,1,0:T(8,128)S(1)} %get-tuple-element.245), kind=kOutput, calls=%fused_computation.15.clone.1 | convolution fusion | flops 171966464 | bytes 17043456 | tf_op jit(solution)/shard_map/while/body/eval_jaxpr/dot_general | solution.py:38
  751.1 25.7 %sqrt_multiply_fusion.2 = f32[256,16384]{0,1:T(8,128)S(1)} fusion(f32[3,256]{1,0:T(4,128)S(1)} %get-tuple-element.282, f32[16384]{0:T(1024)S(1)} %bitcast.109, f32[256]{0:T(256)S(1)} %get-tuple-element.280, f32[1,3,128,128]{3,2,1,0:T(8,128)S(1)} %get-tuple-element.245), kind=kOutput, calls=%fused_computation.15.clone.1 | convolution fusion | flops 171966464 | bytes 17043456 | tf_op jit(solution)/shard_map/while/body/eval_jaxpr/dot_general | solution.py:38
  787.8 25.7 %sqrt_multiply_fusion.2 = f32[256,16384]{0,1:T(8,128)S(1)} fusion(f32[3,256]{1,0:T(4,128)S(1)} %get-tuple-element.282, f32[16384]{0:T(1024)S(1)} %bitcast.109, f32[256]{0:T(256)S(1)} %get-tuple-element.280, f32[1,3,128,128]{3,2,1,0:T(8,128)S(1)} %get-tuple-element.245), kind=kOutput, calls=%fused_computation.15.clone.1 | convolution fusion | flops 171966464 | bytes 17043456 | tf_op jit(solution)/shard_map/while/body/eval_jaxpr/dot_general | solution.py:38
  824.4 25.7 %sqrt_multiply_fusion.2 = f32[256,16384]{0,1:T(8,128)S(1)} fusion(f32[3,256]{1,0:T(4,128)S(1)} %get-tuple-element.282, f32[16384]{0:T(1024)S(1)} %bitcast.109, f32[256]{0:T(256)S(1)} %get-tuple-element.280, f32[1,3,128,128]{3,2,1,0:T(8,128)S(1)} %get-tuple-element.245), kind=kOutput, calls=%fused_computation.15.clone.1 | convolution fusion | flops 171966464 | bytes 17043456 | tf_op jit(solution)/shard_map/while/body/eval_jaxpr/dot_general | solution.py:38
  861.1 25.7 %sqrt_multiply_fusion.2 = f32[256,16384]{0,1:T(8,128)S(1)} fusion(f32[3,256]{1,0:T(4,128)S(1)} %get-tuple-element.282, f32[16384]{0:T(1024)S(1)} %bitcast.109, f32[256]{0:T(256)S(1)} %get-tuple-element.280, f32[1,3,128,128]{3,2,1,0:T(8,128)S(1)} %get-tuple-element.245), kind=kOutput, calls=%fused_computation.15.clone.1 | convolution fusion | flops 171966464 | bytes 17043456 | tf_op jit(solution)/shard_map/while/body/eval_jaxpr/dot_general | solution.py:38
  897.7 25.7 %sqrt_multiply_fusion.2 = f32[256,16384]{0,1:T(8,128)S(1)} fusion(f32[3,256]{1,0:T(4,128)S(1)} %get-tuple-element.282, f32[16384]{0:T(1024)S(1)} %bitcast.109, f32[256]{0:T(256)S(1)} %get-tuple-element.280, f32[1,3,128,128]{3,2,1,0:T(8,128)S(1)} %get-tuple-element.245), kind=kOutput, calls=%fused_computation.15.clone.1 | convolution fusion | flops 171966464 | bytes 17043456 | tf_op jit(solution)/shard_map/while/body/eval_jaxpr/dot_general | solution.py:38
  934.4 25.7 %sqrt_multiply_fusion.2 = f32[256,16384]{0,1:T(8,128)S(1)} fusion(f32[3,256]{1,0:T(4,128)S(1)} %get-tuple-element.282, f32[16384]{0:T(1024)S(1)} %bitcast.109, f32[256]{0:T(256)S(1)} %get-tuple-element.280, f32[1,3,128,128]{3,2,1,0:T(8,128)S(1)} %get-tuple-element.245), kind=kOutput, calls=%fused_computation.15.clone.1 | convolution fusion | flops 171966464 | bytes 17043456 | tf_op jit(solution)/shard_map/while/body/eval_jaxpr/dot_general | solution.py:38
  971.1 25.7 %sqrt_multiply_fusion.2 = f32[256,16384]{0,1:T(8,128)S(1)} fusion(f32[3,256]{1,0:T(4,128)S(1)} %get-tuple-element.282, f32[16384]{0:T(1024)S(1)} %bitcast.109, f32[256]{0:T(256)S(1)} %get-tuple-element.280, f32[1,3,128,128]{3,2,1,0:T(8,128)S(1)} %get-tuple-element.245), kind=kOutput, calls=%fused_computation.15.clone.1 | convolution fusion | flops 171966464 | bytes 17043456 | tf_op jit(solution)/shard_map/while/body/eval_jaxpr/dot_general | solution.py:38
  1007.7 25.7 %sqrt_multiply_fusion.2 = f32[256,16384]{0,1:T(8,128)S(1)} fusion(f32[3,256]{1,0:T(4,128)S(1)} %get-tuple-element.282, f32[16384]{0:T(1024)S(1)} %bitcast.109, f32[256]{0:T(256)S(1)} %get-tuple-element.280, f32[1,3,128,128]{3,2,1,0:T(8,128)S(1)} %get-tuple-element.245), kind=kOutput, calls=%fused_computation.15.clone.1 | convolution fusion | flops 171966464 | bytes 17043456 | tf_op jit(solution)/shard_map/while/body/eval_jaxpr/dot_general | solution.py:38
  1044.4 25.7 %sqrt_multiply_fusion.2 = f32[256,16384]{0,1:T(8,128)S(1)} fusion(f32[3,256]{1,0:T(4,128)S(1)} %get-tuple-element.282, f32[16384]{0:T(1024)S(1)} %bitcast.109, f32[256]{0:T(256)S(1)} %get-tuple-element.280, f32[1,3,128,128]{3,2,1,0:T(8,128)S(1)} %get-tuple-element.245), kind=kOutput, calls=%fused_computation.15.clone.1 | convolution fusion | flops 171966464 | bytes 17043456 | tf_op jit(solution)/shard_map/while/body/eval_jaxpr/dot_general | solution.py:38
  1081.0 25.7 %sqrt_multiply_fusion.2 = f32[256,16384]{0,1:T(8,128)S(1)} fusion(f32[3,256]{1,0:T(4,128)S(1)} %get-tuple-element.282, f32[16384]{0:T(1024)S(1)} %bitcast.109, f32[256]{0:T(256)S(1)} %get-tuple-element.280, f32[1,3,128,128]{3,2,1,0:T(8,128)S(1)} %get-tuple-element.245), kind=kOutput, calls=%fused_computation.15.clone.1 | convolution fusion | flops 171966464 | bytes 17043456 | tf_op jit(solution)/shard_map/while/body/eval_jaxpr/dot_general | solution.py:38
  1116.0 37.6 %psum.7 = f32[3,256]{1,0:T(4,128)S(1)} all-reduce(f32[3,256]{1,0:T(4,128)S(1)} %fusion.41), channel_id=1, replica_groups=mesh['row'=8,'col'=16] {'col'}, use_global_device_ids=true, to_apply=%region_9.10 | all-reduce | flops 768 | bytes 6144 | tf_op jit(solution)/shard_map/psum | solution.py:127
  (142 shorter events, 282.6 us)
Async XLA Ops:
  7.2 56.4 %copy-start = (s32[2,16384]{1,0:T(2,128)S(1)}, s32[2,16384]{1,0:T(2,128)}, u32[]{:S(2)}) copy-start(s32[2,16384]{1,0:T(2,128)} %param.6) | copy-start | bytes 393220
  28.0 163.8 %all-to-all-start = ((f32[3,256,128]{2,0,1:T(4,128)}), f32[3,256,128]{2,0,1:T(4,128)S(1)}, u32[]{:S(2)}, u32[]{:S(2)}) async-start(f32[3,256,128]{2,0,1:T(4,128)} %scatter_fusion), calls=%async_computation | async-start | bytes 1048576 | tf_op jit(solution)/shard_map/all_to_all | solution.py:95
  39.1 417.4 %all-gather.3.cloned.1.call-start = ((), (), s32[]{:S(2)}) async-start(), calls=%async_computation.1 | async-start | bytes 4227072 | tf_op jit(solution)/shard_map/all_gather | solution.py:118
  257.2 271.6 %all-gather.5.cloned.1.call-start = ((), (), s32[]{:S(2)}) async-start(), calls=%async_computation.2 | async-start | bytes 7077888 | tf_op jit(solution)/shard_map/all_gather | solution.py:125
Sparse Core Ops, SparseCore 0:
  257.3 199.1 all-gather.2
  458.1 70.5 all-gather.4
